TPU v7x, 32 devices: a whole 2x2x4 slice. The times are simulated.
32 devices in a mesh: row: 2 (over x), col: 4 (over y, core), mode: 4 (over z).
Axes of the slice: x: 2, y: 2, z: 4, core: 2. Of those that a mesh axis runs over, the one named last changes fastest.
Arguments:
- object_field: float32 [2, 512, 1024], P(None, 'row', 'col'), may hold values from -6 to 6
- probe_real: float32 [4, 128, 128], P('mode'), may hold values from -3 to 3
- probe_imag: float32 [4, 128, 128], P('mode'), may hold values from -3 to 3
- amplitude: float32 [2, 4, 8, 128, 128], P('row', 'col'), may hold values from 0 to 3
- positions: int32 [2, 4, 8, 2], P('row', 'col'), may hold values from 0 to 256, as said below
- counts: int32 [2, 4], P('row', 'col'), may hold values from 2 to 8, as said below
Outputs:
- updated: float32 [2, 512, 1024], P(None, 'row', 'col')
Inputs may be any that keep to these rules, and one draw needn't show every extreme that they name: `positions`: offsets lie in 0 to 256 for rows and 0 to 256 for columns. In every tile slot 0 starts within the first 64 rows and columns of the window, and slot 1 ends within the last 64 rows and columns. `counts`: some tile has 8 frames and some tile has 2.
All inputs are finite; a program needn't handle non-finite values.
Results may differ from a plain program's by a relative error of at most 0.0003.
Values sent between devices are 32-bit elements; how exact they have to be, the bound alone decides.
A program may use at most 64 MiB of HBM per device.

v0:
```python
from functools import partial

import jax
import jax.numpy as jnp
from jax import lax
from jax.sharding import PartitionSpec as P

FRAME = 128
MARGIN = 64
SLOTS = 8


STEP_SIZE = 0.25


def padded(cells, sides, width):
    for axis, dim in sides:
        count = lax.axis_size(axis)
        ends = count - 1
        head = lax.slice_in_dim(cells, 0, width, axis=dim)
        tail = lax.slice_in_dim(cells, cells.shape[dim] - width, cells.shape[dim], axis=dim)
        cells = jnp.concatenate(
            [
                lax.ppermute(tail, axis, [(i, (i + 1) % count) for i in range(ends)]),
                cells,
                lax.ppermute(head, axis, [((i + 1) % count, i) for i in range(ends)]),
            ],
            axis=dim,
        )
    return cells


def tables(length):
    counter = jnp.arange(length, dtype=jnp.int32)
    phase = counter[:, None] * counter[None, :] % length
    angles = phase.astype(jnp.float32) * (2.0 * jnp.pi / length)
    factor = 1.0 / jnp.sqrt(jnp.float32(length))
    return (jnp.cos(angles) * factor, jnp.sin(angles) * factor)


def transform(real_part, imag_part, cosine, sine_table, direction):
    product = partial(jnp.matmul, precision=lax.Precision.HIGHEST)
    left_real = product(cosine, real_part) + direction * product(sine_table, imag_part)
    left_imag = product(cosine, imag_part) - direction * product(sine_table, real_part)
    out_real = product(left_real, cosine) + direction * product(left_imag, sine_table)
    out_imag = product(left_imag, cosine) - direction * product(left_real, sine_table)
    return (out_real, out_imag)


def forward_wave(window, mode_real, mode_imag, cosine, sine_table):
    object_real = window[..., 0, :, :]
    object_imag = window[..., 1, :, :]
    wave_real = mode_real * object_real - mode_imag * object_imag
    wave_imag = mode_real * object_imag + mode_imag * object_real
    return transform(wave_real, wave_imag, cosine, sine_table, 1.0)


def backward_wave(
    spec_real, spec_imag, intensity, target, mode_real, mode_imag, cosine, sine_table
):
    keep = 1.0 - target / jnp.maximum(jnp.sqrt(intensity), 1.0)
    back_real, back_imag = transform(spec_real * keep, spec_imag * keep, cosine, sine_table, -1.0)
    grad_real = mode_real * back_real + mode_imag * back_imag
    grad_imag = mode_real * back_imag - mode_imag * back_real
    return jnp.stack([grad_real, grad_imag], axis=-3)


def fold_rims(gradient):
    margin = MARGIN
    borders = jnp.concatenate([gradient[:, :margin], gradient[:, -margin:]], axis=1)
    received = padded(borders, (("row", 1),), margin)
    interior = gradient[:, margin:-margin]
    interior = interior.at[:, :margin].add(received[:, :margin])
    interior = interior.at[:, -margin:].add(received[:, -margin:])
    sideways = jnp.concatenate([interior[:, :, :margin], interior[:, :, -margin:]], axis=2)
    arrived = padded(sideways, (("col", 2),), margin)
    centre = interior[:, :, margin:-margin]
    centre = centre.at[:, :, :margin].add(arrived[:, :, :margin])
    centre = centre.at[:, :, -margin:].add(arrived[:, :, -margin:])
    return centre


def per_device(object_field, probe_real, probe_imag, amplitude, positions, counts):
    cosine, sine_table = tables(FRAME)
    extended = padded(object_field, (("row", 1), ("col", 2)), MARGIN)
    measured = amplitude[0, 0]
    offsets = positions[0, 0]
    active = counts[0, 0]
    anchor = jnp.zeros((), jnp.int32)

    def window_of(slot):
        return lax.dynamic_slice(
            extended, (anchor, offsets[slot, 0], offsets[slot, 1]), (2, FRAME, FRAME)
        )

    def deposit(gradient, slot, contrib):
        weight = (slot < active).astype(jnp.float32)
        corner = (anchor, offsets[slot, 0], offsets[slot, 1])
        previous = lax.dynamic_slice(gradient, corner, (2, FRAME, FRAME))
        return lax.dynamic_update_slice(gradient, previous + contrib * weight, corner)

    gradient = jnp.zeros(extended.shape, jnp.float32)
    all_real, all_imag = (
        lax.all_gather(probe_real, "mode", axis=0, tiled=True),
        lax.all_gather(probe_imag, "mode", axis=0, tiled=True),
    )
    member = lax.axis_index("mode")
    group = lax.axis_size("mode")

    def advance_own(turn, gradient):
        slot = member + turn * group
        spec_real, spec_imag = forward_wave(window_of(slot), all_real, all_imag, cosine, sine_table)
        intensity = jnp.sum(spec_real * spec_real + spec_imag * spec_imag, axis=0)
        terms = backward_wave(
            spec_real, spec_imag, intensity, measured[slot], all_real, all_imag, cosine, sine_table
        )
        return deposit(gradient, slot, jnp.sum(terms, axis=0))

    gradient = lax.fori_loop(0, SLOTS // group, advance_own, gradient)
    summed = lax.psum(gradient, "mode")
    total = fold_rims(summed)
    return object_field - STEP_SIZE * total


def solution(mesh):
    in_specs = (
        P(None, "row", "col"),
        P("mode", None, None),
        P("mode", None, None),
        P("row", "col", None, None, None),
        P("row", "col", None, None),
        P("row", "col"),
    )
    out_specs = P(None, "row", "col")
    return jax.shard_map(
        per_device, mesh=mesh, in_specs=in_specs, out_specs=out_specs, check_vma=False
    )
```

profile of v0, /device:TPU:1, one launch (start us, length us, event | category | flops | bytes accessed | tf_op | source)
XLA Modules:
  0.0 185.6 jit_solution(7516222423846577421)
XLA Ops:
  7.5 3.9 %collective-permute-start = (f32[2,64,256]{2,1,0:T(8,128)S(1)}, f32[2,64,256]{2,1,0:T(8,128)S(1)}, u32[]{:S(2)}, u32[]{:S(2)}) collective-permute-start(f32[2,64,256]{2,1,0:T(8,128)S(1)} %get-tuple-element.375), channel_id=1, source_target_pairs={{0,16},{1,17},{2,18},{3,19},{4,20},{5,21},{6,22},{7,23},{8,24},{9,... | collective-permute-start | bytes 393224 | tf_op jit(solution)/shard_map/ppermute | solution.py:24
  11.5 1.3 collective-permute-start.1
  13.6 1.1 constant_dynamic-update-slice_fusion.1
  14.8 2.4 %collective-permute-done.1 = f32[2,64,256]{2,1,0:T(8,128)S(1)} collective-permute-done((f32[2,64,256]{2,1,0:T(8,128)S(1)}, f32[2,64,256]{2,1,0:T(8,128)S(1)}, u32[]{:S(2)}, u32[]{:S(2)}) %collective-permute-start.1) | collective-permute-done | bytes 131104 | tf_op jit(solution)/shard_map/ppermute | solution.py:26
  17.4 5.1 %collective-permute-start.2 = (f32[2,384,64]{2,1,0:T(8,128)S(1)}, f32[2,384,64]{2,1,0:T(8,128)S(1)}, u32[]{:S(2)}, u32[]{:S(2)}) collective-permute-start(f32[2,384,64]{2,1,0:T(8,128)S(1)} %get-tuple-element.372), channel_id=1, source_target_pairs={{0,4},{4,8},{8,12},{1,5},{5,9},{9,13},{2,6},{6,10},{10,14},{3,7},{... | collective-permute-start | bytes 589832 | tf_op jit(solution)/shard_map/ppermute | solution.py:24
  22.5 1.9 %collective-permute-start.3 = (f32[2,384,64]{2,1,0:T(8,128)S(1)}, f32[2,384,64]{2,1,0:T(8,128)S(1)}, u32[]{:S(2)}, u32[]{:S(2)}) collective-permute-start(f32[2,384,64]{2,1,0:T(8,128)S(1)} %get-tuple-element.373), channel_id=1, source_target_pairs={{4,0},{8,4},{12,8},{5,1},{9,5},{13,9},{6,2},{10,6},{14,10},{7,3},{... | collective-permute-start | bytes 589832 | tf_op jit(solution)/shard_map/ppermute | solution.py:26
  24.5 12.1 %all_gather.6 = f32[4,128,128]{2,1,0:T(8,128)S(1)} all-gather(f32[1,128,128]{2,1,0:T(8,128)S(1)} %copy-done.3), channel_id=1, replica_groups=mesh['row'=2,'col'=4,'mode'=4] {'mode'}, dimensions={0}, use_global_device_ids=true | all-gather | bytes 327680 | tf_op jit(solution)/shard_map/all_gather | solution.py:104
  36.5 12.3 %all_gather.7 = f32[4,128,128]{2,1,0:T(8,128)S(1)} all-gather(f32[1,128,128]{2,1,0:T(8,128)S(1)} %copy-done.4), channel_id=1, replica_groups=mesh['row'=2,'col'=4,'mode'=4] {'mode'}, dimensions={0}, use_global_device_ids=true | all-gather | bytes 327680 | tf_op jit(solution)/shard_map/all_gather | solution.py:105
  50.0 40.9 %while.19 = (s32[]{:T(128)}, f32[2,384,384]{2,1,0:T(8,128)S(1)}, s32[]{:T(128)}, s32[8,2]{0,1:T(2,128)S(1)}, f32[2,384,384]{2,1,0:T(8,128)S(1)}, /*index=5*/f32[...) while((s32[]{:T(128)}, f32[2,384,384]{2,1,0:T(8,128)S(1)}, ...), condition=%wide.region_3.4_spmd.clone.clone, body=%wide.region_0.3_spmd.clone.clone.sunk | while | flops 1617362944 | bytes 15466841 | solution.py:119
  67.9 2.5 %dynamic_update_slice.10 = f32[2,384,384]{2,1,0:T(8,128)S(1)} dynamic-update-slice(f32[2,384,384]{2,1,0:T(8,128)S(1)} %get-tuple-element.463, f32[2,128,128]{2,1,0:T(8,128)S(1)} %multiply_add_fusion.9, s32[]{:T(128)} %constant.176.clone.1..sunk, s32[]{:T(128)S(6)} %select_n.178, s32[]{:T(128)S(6)} %select_n.179) | dynamic-update-slice | bytes 262148 | tf_op jit(solution)/shard_map/while/body/eval_jaxpr/dynamic_update_slice | solution.py:100
  88.3 2.5 %dynamic_update_slice.10 = f32[2,384,384]{2,1,0:T(8,128)S(1)} dynamic-update-slice(f32[2,384,384]{2,1,0:T(8,128)S(1)} %get-tuple-element.463, f32[2,128,128]{2,1,0:T(8,128)S(1)} %multiply_add_fusion.9, s32[]{:T(128)} %constant.176.clone.1..sunk, s32[]{:T(128)S(6)} %select_n.178, s32[]{:T(128)S(6)} %select_n.179) | dynamic-update-slice | bytes 262148 | tf_op jit(solution)/shard_map/while/body/eval_jaxpr/dynamic_update_slice | solution.py:100
  90.9 1.0 copy-done
  91.9 59.9 %all-reduce.2.cloned.1.call-done = f32[2,384,384]{2,1,0:T(8,128)} async-done(((f32[2,384,384]{2,1,0:T(8,128)}), f32[2,384,384]{2,1,0:T(8,128)}) %all-reduce.2.cloned.1.call-update) | async-done | bytes 1179664 | tf_op jit(solution)/shard_map/psum | solution.py:120
  151.8 1.2 fusion.134
  153.0 3.1 %collective-permute-start.4 = (f32[2,64,384]{2,1,0:T(8,128)S(1)}, f32[2,64,384]{2,1,0:T(8,128)S(1)}, u32[]{:S(2)}, u32[]{:S(2)}) collective-permute-start(f32[2,64,384]{2,1,0:T(8,128)S(1)} %get-tuple-element.369), channel_id=1, source_target_pairs={{0,16},{1,17},{2,18},{3,19},{4,20},{5,21},{6,22},{7,23},{8,24},{9,... | collective-permute-start | bytes 589832 | tf_op jit(solution)/shard_map/ppermute | solution.py:24
  156.1 1.3 collective-permute-start.5
  157.4 2.4 %collective-permute-done.4 = f32[2,64,384]{2,1,0:T(8,128)S(1)} collective-permute-done((f32[2,64,384]{2,1,0:T(8,128)S(1)}, f32[2,64,384]{2,1,0:T(8,128)S(1)}, u32[]{:S(2)}, u32[]{:S(2)}) %collective-permute-start.4) | collective-permute-done | bytes 196640 | tf_op jit(solution)/shard_map/ppermute | solution.py:24
  159.8 3.8 %collective-permute-done.5 = f32[2,64,384]{2,1,0:T(8,128)S(1)} collective-permute-done((f32[2,64,384]{2,1,0:T(8,128)S(1)}, f32[2,64,384]{2,1,0:T(8,128)S(1)}, u32[]{:S(2)}, u32[]{:S(2)}) %collective-permute-start.5) | collective-permute-done | bytes 196640 | tf_op jit(solution)/shard_map/ppermute | solution.py:26
  163.8 4.7 %collective-permute-start.6 = (f32[2,256,64]{2,1,0:T(8,128)S(1)}, f32[2,256,64]{2,1,0:T(8,128)S(1)}, u32[]{:S(2)}, u32[]{:S(2)}) collective-permute-start(f32[2,256,64]{2,1,0:T(8,128)S(1)} %get-tuple-element.371), channel_id=1, source_target_pairs={{0,4},{4,8},{8,12},{1,5},{5,9},{9,13},{2,6},{6,10},{10,14},{3,7},{... | collective-permute-start | bytes 393224 | tf_op jit(solution)/shard_map/ppermute | solution.py:24
  168.7 2.1 %collective-permute-start.7 = (f32[2,256,64]{2,1,0:T(8,128)S(1)}, f32[2,256,64]{2,1,0:T(8,128)S(1)}, u32[]{:S(2)}, u32[]{:S(2)}) collective-permute-start(f32[2,256,64]{2,1,0:T(8,128)S(1)} %get-tuple-element.370), channel_id=1, source_target_pairs={{4,0},{8,4},{12,8},{5,1},{9,5},{13,9},{6,2},{10,6},{14,10},{7,3},{... | collective-permute-start | bytes 393224 | tf_op jit(solution)/shard_map/ppermute | solution.py:26
  170.8 1.0 collective-permute-done.6
  171.9 1.1 scatter-add.16
  173.1 3.5 %collective-permute-done.7 = f32[2,256,64]{2,1,0:T(8,128)S(1)} collective-permute-done((f32[2,256,64]{2,1,0:T(8,128)S(1)}, f32[2,256,64]{2,1,0:T(8,128)S(1)}, u32[]{:S(2)}, u32[]{:S(2)}) %collective-permute-start.7) | collective-permute-done | bytes 131104 | tf_op jit(solution)/shard_map/ppermute | solution.py:26
  176.7 1.2 scatter-add.19
  (73 shorter events, 31.9 us)
Async XLA Ops:
  6.5 145.3 %all-reduce.2.cloned.1.call-start = ((), (), s32[]{:S(2)}) async-start(), calls=%async_computation | async-start | bytes 2359296 | tf_op jit(solution)/shard_map/psum | solution.py:120
  7.5 6.1 %collective-permute-start = (f32[2,64,256]{2,1,0:T(8,128)S(1)}, f32[2,64,256]{2,1,0:T(8,128)S(1)}, u32[]{:S(2)}, u32[]{:S(2)}) collective-permute-start(f32[2,64,256]{2,1,0:T(8,128)S(1)} %get-tuple-element.375), channel_id=1, source_target_pairs={{0,16},{1,17},{2,18},{3,19},{4,20},{5,21},{6,22},{7,23},{8,24},{9,... | collective-permute-start | bytes 393224 | tf_op jit(solution)/shard_map/ppermute | solution.py:24
  11.5 5.7 %collective-permute-start.1 = (f32[2,64,256]{2,1,0:T(8,128)S(1)}, f32[2,64,256]{2,1,0:T(8,128)S(1)}, u32[]{:S(2)}, u32[]{:S(2)}) collective-permute-start(f32[2,64,256]{2,1,0:T(8,128)S(1)} %get-tuple-element.374), channel_id=1, source_target_pairs={{16,0},{17,1},{18,2},{19,3},{20,4},{21,5},{22,6},{23,7},{24,8},{25... | collective-permute-start | bytes 393224 | tf_op jit(solution)/shard_map/ppermute | solution.py:26
  14.7 9.7 %copy-start.3 = (f32[1,128,128]{2,1,0:T(8,128)S(1)}, f32[1,128,128]{2,1,0:T(8,128)}, u32[]{:S(2)}) copy-start(f32[1,128,128]{2,1,0:T(8,128)} %param.17) | copy-start | bytes 196612
  14.7 21.8 %copy-start.4 = (f32[1,128,128]{2,1,0:T(8,128)S(1)}, f32[1,128,128]{2,1,0:T(8,128)}, u32[]{:S(2)}) copy-start(f32[1,128,128]{2,1,0:T(8,128)} %param.18) | copy-start | bytes 196612
  17.4 31.4 %collective-permute-start.2 = (f32[2,384,64]{2,1,0:T(8,128)S(1)}, f32[2,384,64]{2,1,0:T(8,128)S(1)}, u32[]{:S(2)}, u32[]{:S(2)}) collective-permute-start(f32[2,384,64]{2,1,0:T(8,128)S(1)} %get-tuple-element.372), channel_id=1, source_target_pairs={{0,4},{4,8},{8,12},{1,5},{5,9},{9,13},{2,6},{6,10},{10,14},{3,7},{... | collective-permute-start | bytes 589832 | tf_op jit(solution)/shard_map/ppermute | solution.py:24
  22.5 26.3 %collective-permute-start.3 = (f32[2,384,64]{2,1,0:T(8,128)S(1)}, f32[2,384,64]{2,1,0:T(8,128)S(1)}, u32[]{:S(2)}, u32[]{:S(2)}) collective-permute-start(f32[2,384,64]{2,1,0:T(8,128)S(1)} %get-tuple-element.373), channel_id=1, source_target_pairs={{4,0},{8,4},{12,8},{5,1},{9,5},{13,9},{6,2},{10,6},{14,10},{7,3},{... | collective-permute-start | bytes 589832 | tf_op jit(solution)/shard_map/ppermute | solution.py:26
  49.3 0.7 copy-start.5
  90.8 1.0 copy-start
  151.8 8.0 %copy-start.1 = (f32[2,384,384]{2,1,0:T(8,128)S(1)}, f32[2,384,384]{2,1,0:T(8,128)}, u32[]{:S(2)}) copy-start(f32[2,384,384]{2,1,0:T(8,128)} %all-reduce.2.cloned.1.call-done) | copy-start | bytes 3538948
  151.8 8.0 %slice-start = ((f32[2,384,384]{2,1,0:T(8,128)}), f32[2,256,384]{2,1,0:T(8,128)S(1)}, s32[]{:S(2)}) async-start(f32[2,384,384]{2,1,0:T(8,128)} %all-reduce.2.cloned.1.call-done), calls=%async_computation.1 | async-start | bytes 1572864 | tf_op jit(solution)/shard_map/slice | solution.py:72
  153.0 6.8 %collective-permute-start.4 = (f32[2,64,384]{2,1,0:T(8,128)S(1)}, f32[2,64,384]{2,1,0:T(8,128)S(1)}, u32[]{:S(2)}, u32[]{:S(2)}) collective-permute-start(f32[2,64,384]{2,1,0:T(8,128)S(1)} %get-tuple-element.369), channel_id=1, source_target_pairs={{0,16},{1,17},{2,18},{3,19},{4,20},{5,21},{6,22},{7,23},{8,24},{9,... | collective-permute-start | bytes 589832 | tf_op jit(solution)/shard_map/ppermute | solution.py:24
  156.1 7.5 %collective-permute-start.5 = (f32[2,64,384]{2,1,0:T(8,128)S(1)}, f32[2,64,384]{2,1,0:T(8,128)S(1)}, u32[]{:S(2)}, u32[]{:S(2)}) collective-permute-start(f32[2,64,384]{2,1,0:T(8,128)S(1)} %get-tuple-element.368), channel_id=1, source_target_pairs={{16,0},{17,1},{18,2},{19,3},{20,4},{21,5},{22,6},{23,7},{24,8},{25... | collective-permute-start | bytes 589832 | tf_op jit(solution)/shard_map/ppermute | solution.py:26
  163.8 8.0 %collective-permute-start.6 = (f32[2,256,64]{2,1,0:T(8,128)S(1)}, f32[2,256,64]{2,1,0:T(8,128)S(1)}, u32[]{:S(2)}, u32[]{:S(2)}) collective-permute-start(f32[2,256,64]{2,1,0:T(8,128)S(1)} %get-tuple-element.371), channel_id=1, source_target_pairs={{0,4},{4,8},{8,12},{1,5},{5,9},{9,13},{2,6},{6,10},{10,14},{3,7},{... | collective-permute-start | bytes 393224 | tf_op jit(solution)/shard_map/ppermute | solution.py:24
  168.7 9.2 %copy-start.2 = (f32[2,256,256]{2,1,0:T(8,128)S(1)}, f32[2,256,256]{2,1,0:T(8,128)}, u32[]{:S(2)}) copy-start(f32[2,256,256]{2,1,0:T(8,128)} %param.16) | copy-start | bytes 1572868
  168.7 7.8 %collective-permute-start.7 = (f32[2,256,64]{2,1,0:T(8,128)S(1)}, f32[2,256,64]{2,1,0:T(8,128)S(1)}, u32[]{:S(2)}, u32[]{:S(2)}) collective-permute-start(f32[2,256,64]{2,1,0:T(8,128)S(1)} %get-tuple-element.370), channel_id=1, source_target_pairs={{4,0},{8,4},{12,8},{5,1},{9,5},{13,9},{6,2},{10,6},{14,10},{7,3},{... | collective-permute-start | bytes 393224 | tf_op jit(solution)/shard_map/ppermute | solution.py:26
Sparse Core Ops, SparseCore 0:
  92.0 59.7 all-reduce.1
where the time goes:
time: 186 us
  waiting for transfers between devices  73.9 us (40%)
  blocking collectives  24.4 us (13%)
  matrix products  23.7 us (13%)
  starting transfers between devices  23.4 us (13%)
  local copies, waits for them, and re-layouts  14.2 us (8%)
  between operations  13.6 us (7%)
  loops' own time  8.74 us (5%)
  other arithmetic  3.71 us (2%)
    psum x1, waiting for transfers between devices, per_device(): summed = lax.psum(gradient, 'mode')  59.9 us
    ppermute x4, starting transfers between devices, padded(): lax.ppermute(tail, axis, [(i, (i + 1) % count) for i in range(ends)])  16.9 us
    all_gather x1, blocking collectives, per_device(): lax.all_gather(probe_imag, 'mode', axis=0, tiled=True)  12.3 us
    all_gather x1, blocking collectives, per_device(): lax.all_gather(probe_real, 'mode', axis=0, tiled=True)  12.1 us
    ppermute x4, waiting for transfers between devices, padded(): lax.ppermute(head, axis, [((i + 1) % count, i) for i in range(ends)])  9.72 us
    another operation x1, loops' own time, per_device(): gradient = lax.fori_loop(0, SLOTS // group, advance_own, gradient)  8.74 us
    ppermute x4, starting transfers between devices, padded(): lax.ppermute(head, axis, [((i + 1) % count, i) for i in range(ends)])  6.56 us
    dynamic_update_slice x2, local copies, waits for them, and re-layouts, deposit(): lax.dynamic_update_slice(gradient, previous + contrib * weight, corner)  4.99 us
  transfers between devices with their start and end apart: 9, of which 7 were waited for; matrix products, arithmetic and copies ran while one was open for 1% of the time, Pallas kernels for 0%

commit v1 on v0

v1 whole, which is shorter than its diff:
```python
import functools

import jax
import jax.numpy as jnp
import numpy as np
from jax import lax
from jax.experimental import pallas as pl
from jax.experimental.pallas import tpu as pltpu
from jax.sharding import PartitionSpec as P

MARGIN = 64
LANES = 128
SUBLANES = 8
STEP_SIZE = 0.25
MESH_ID = pl.DeviceIdType.MESH

DIRS = ((-1, 0), (1, 0), (0, -1), (0, 1), (-1, -1), (-1, 1), (1, -1), (1, 1))
OPP = tuple(DIRS.index((-a, -b)) for a, b in DIRS)


def dft_tables(length):
    k = np.arange(length)
    angle = 2.0 * np.pi * (np.outer(k, k) % length) / length
    c = np.cos(angle) / np.sqrt(length)
    s = np.sin(angle) / np.sqrt(length)
    plus = np.block([[c, s], [-s, c]])
    minus = np.block([[c, -s], [s, c]])

    def split(t):
        hi = t.astype(jnp.bfloat16)
        lo = (t - hi.astype(np.float64)).astype(jnp.bfloat16)
        return hi, lo

    ph, pw = split(plus)
    mh, mw = split(minus)
    right_f = np.concatenate([mh, mh, mw], axis=0)
    left_f = np.concatenate([ph, ph, pw], axis=1)
    left_b = np.concatenate([mh, mh, mw], axis=1)
    right_b = np.concatenate([ph, ph, pw], axis=0)
    return right_f, left_f, left_b, right_b


def neighbour_flags():
    row, col = lax.axis_index("row"), lax.axis_index("col")
    rows, cols = lax.axis_size("row"), lax.axis_size("col")
    flags = []
    for a, b in DIRS:
        r, c = row + a, col + b
        ok = jnp.logical_and(jnp.logical_and(r >= 0, r < rows), jnp.logical_and(c >= 0, c < cols))
        flags.append(ok)
    return flags


def target(step):
    return (lax.axis_index("row") + step[0], lax.axis_index("col") + step[1], lax.axis_index("mode"))


def enter(flags, others):
    barrier = pltpu.get_barrier_semaphore()
    total = jnp.int32(len(others))
    for flag, step in zip(flags, DIRS):
        total = total + flag.astype(jnp.int32)

        @pl.when(flag)
        def _():
            pl.semaphore_signal(barrier, inc=1, device_id=target(step), device_id_type=MESH_ID)

    for device in others:
        pl.semaphore_signal(barrier, inc=1, device_id=device, device_id_type=MESH_ID)
    pl.semaphore_wait(barrier, total)


def rim_copies(parts, slots, send, recv):
    return [
        pltpu.make_async_remote_copy(
            src_ref=parts[i], dst_ref=slots[i], send_sem=send.at[i], recv_sem=recv.at[i],
            device_id=target(DIRS[i]), device_id_type=MESH_ID,
        )
        for i in range(len(DIRS))
    ]


def gather_kernel(
    modes, cols, obj, pr, pi, halo_row, halo_col, halo_corner, others,
    send, recv, psend, precv, fsend, frecv,
):
    row, col, mode = lax.axis_index("row"), lax.axis_index("col"), lax.axis_index("mode")
    height, width = obj.shape[1], obj.shape[2]
    flags = neighbour_flags()
    parity = col % 2
    paired = cols % 2 == 0
    partner = col + 1 - 2 * parity
    peers = [(row, col, (mode + k) % modes) for k in range(1, modes)]
    enter(flags, peers)

    sides = (0, 1) if not paired else (None,)

    def probe_copy(k, side):
        source = (pr, pi)[side]
        return pltpu.make_async_remote_copy(
            src_ref=source.at[0], dst_ref=others.at[k, side], send_sem=psend.at[k, side],
            recv_sem=precv.at[k, side], device_id=peers[k], device_id_type=MESH_ID,
        )

    def forward_copy(k, side):
        return pltpu.make_async_remote_copy(
            src_ref=others.at[k, side], dst_ref=others.at[k, side], send_sem=fsend.at[k, side],
            recv_sem=frecv.at[k, side], device_id=(row, partner, mode), device_id_type=MESH_ID,
        )

    for k in reversed(range(modes - 1)):
        for side in (0, 1):
            if paired:
                @pl.when(parity == side)
                def _():
                    probe_copy(k, side).start()
            else:
                probe_copy(k, side).start()

    bands = [pl.ds(0, MARGIN), pl.ds(height - MARGIN, MARGIN)]
    strips = [pl.ds(0, LANES), pl.ds(width - LANES, LANES)]
    parts, slots = [], []
    for a, b in DIRS:
        rs = pl.ds(0, height) if a == 0 else bands[(a + 1) // 2]
        cs = pl.ds(0, width) if b == 0 else strips[(b + 1) // 2]
        parts.append(obj.at[:, rs, cs])
        ia, ib = (1 - a) // 2, (1 - b) // 2
        if b == 0:
            slots.append(halo_row.at[ia])
        elif a == 0:
            slots.append(halo_col.at[ib])
        else:
            slots.append(halo_corner.at[ia * 2 + ib])
    copies = rim_copies(parts, slots, send, recv)
    for i in range(len(DIRS)):
        @pl.when(flags[i])
        def _():
            copies[i].start()

    if paired:
        for k in range(modes - 1):
            for side in (0, 1):
                @pl.when(parity == side)
                def _():
                    probe_copy(k, side).wait_recv()
                    forward_copy(k, side).start()
        for k in range(modes - 1):
            for side in (0, 1):
                @pl.when(parity == side)
                def _():
                    probe_copy(k, side).wait_send()
                    forward_copy(k, side).wait_send()
                    forward_copy(k, 1 - side).wait_recv()
    else:
        for k in range(modes - 1):
            for side in (0, 1):
                probe_copy(k, side).wait()
    for i in range(len(DIRS)):
        @pl.when(flags[i])
        def _():
            copies[i].wait_send()

        @pl.when(flags[OPP[i]])
        def _():
            copies[i].wait_recv()


def gather(obj, pr, pi):
    modes, cols = lax.axis_size("mode"), lax.axis_size("col")
    _, height, width = obj.shape
    frame = pr.shape[-1]
    f32 = jnp.float32
    sem = pltpu.SemaphoreType.DMA
    return pl.pallas_call(
        functools.partial(gather_kernel, modes, cols),
        out_shape=[
            jax.ShapeDtypeStruct((2, 2, MARGIN, width), f32),
            jax.ShapeDtypeStruct((2, 2, height, LANES), f32),
            jax.ShapeDtypeStruct((4, 2, MARGIN, LANES), f32),
            jax.ShapeDtypeStruct((modes - 1, 2, frame, frame), f32),
        ],
        in_specs=[pl.BlockSpec(memory_space=pl.ANY)] * 3,
        out_specs=[pl.BlockSpec(memory_space=pl.ANY)] * 4,
        scratch_shapes=[
            sem((8,)), sem((8,)),
            sem((modes - 1, 2)), sem((modes - 1, 2)),
            sem((modes - 1, 2)), sem((modes - 1, 2)),
        ],
        compiler_params=pltpu.CompilerParams(collective_id=0, has_side_effects=True),
        name="gather",
    )(obj, pr, pi)


def split(x):
    hi = x.astype(jnp.bfloat16)
    lo = (x - hi.astype(jnp.float32)).astype(jnp.bfloat16)
    return hi, lo


def apply_right(x, table):
    hi, lo = split(x)
    return jnp.dot(
        jnp.concatenate([hi, lo, hi], axis=1), table, preferred_element_type=jnp.float32
    )


def apply_left(table, x):
    hi, lo = split(x)
    return jnp.dot(
        table, jnp.concatenate([hi, lo, hi], axis=0), preferred_element_type=jnp.float32
    )


def frames_kernel(
    modes, pos, cnt, obj, halo_row, halo_col, halo_corner, pr, pi, others, amp, rf, lf, lb, rb,
    acc, win, probe, tgt, sems, asems,
):
    height, width = obj.shape[1], obj.shape[2]
    frame = pr.shape[-1]
    rows, cols = win.shape[1], win.shape[2]
    slots = amp.shape[2]
    tall = frame + SUBLANES
    flags = neighbour_flags()
    center = (pl.ds(0, 2), pl.ds(MARGIN, height), pl.ds(LANES, width))

    loads = [
        (obj, win.at[center]),
        (obj, acc.at[center]),
        (pr.at[0], probe.at[0, 0]),
        (pi.at[0], probe.at[0, 1]),
    ]
    copies = [pltpu.make_async_copy(s, d, sems.at[i]) for i, (s, d) in enumerate(loads)]
    copies.append(
        pltpu.make_async_copy(others, probe.at[pl.ds(1, modes - 1)], sems.at[len(loads)])
    )
    for copy in copies:
        copy.start()
    targets = [pltpu.make_async_copy(amp.at[0, 0], tgt, asems.at[0])]
    for copy in targets:
        copy.start()

    acc[:, pl.ds(0, MARGIN), :] = jnp.zeros((2, MARGIN, cols), jnp.float32)
    acc[:, pl.ds(MARGIN + height, MARGIN), :] = jnp.zeros((2, MARGIN, cols), jnp.float32)
    acc[:, pl.ds(MARGIN, height), pl.ds(0, LANES)] = jnp.zeros((2, height, LANES), jnp.float32)
    acc[:, pl.ds(MARGIN, height), pl.ds(LANES + width, LANES)] = jnp.zeros(
        (2, height, LANES), jnp.float32
    )

    base = len(copies)
    for i, (a, b) in enumerate(DIRS):
        rs = (pl.ds(0, MARGIN), pl.ds(MARGIN, height), pl.ds(MARGIN + height, MARGIN))[a + 1]
        cs = (pl.ds(0, LANES), pl.ds(LANES, width), pl.ds(LANES + width, LANES))[b + 1]
        ia, ib = (a + 1) // 2, (b + 1) // 2
        if b == 0:
            source = halo_row.at[ia]
        elif a == 0:
            source = halo_col.at[ib]
        else:
            source = halo_corner.at[ia * 2 + ib]
        place = win.at[:, rs, cs]
        copy = pltpu.make_async_copy(source, place, sems.at[base + i])

        @pl.when(flags[i])
        def _():
            copy.start()

        @pl.when(jnp.logical_not(flags[i]))
        def _():
            place[...] = jnp.zeros(place.shape, jnp.float32)

        copies.append(copy)

    for copy in copies[:base]:
        copy.wait()
    for i in range(len(DIRS)):
        @pl.when(flags[i])
        def _():
            copies[base + i].wait()
    for copy in targets:
        copy.wait()

    def window_of(top, lift, first, shift):
        out = []
        for part in range(2):
            wide = win[part, pl.ds(top, tall), pl.ds(first, 2 * LANES)]
            wide = pltpu.roll(wide, shift, axis=1)[:, :frame]
            out.append(pltpu.roll(wide, (tall - lift) % tall, axis=0)[:frame])
        return out

    def place_of(slot):
        a = pos[0, 0, slot, 0]
        b = pos[0, 0, slot, 1] + (LANES - MARGIN)
        q = lax.div(b, LANES)
        top = lax.div(a, SUBLANES)
        lift = a - top * SUBLANES
        return pl.multiple_of(top * SUBLANES, SUBLANES), lift, pl.multiple_of(q * LANES, LANES), b - q * LANES

    def contribution(slot):
        top, lift, first, rest = place_of(slot)
        re, im = window_of(top, lift, first, (2 * LANES - rest) % (2 * LANES))
        waves = []
        for m in range(modes):
            p, q = probe[m, 0], probe[m, 1]
            waves.append(jnp.concatenate([p * re - q * im, p * im + q * re], axis=1))
        z = apply_right(jnp.concatenate(waves, axis=0), rf[...])
        z = jnp.concatenate(
            [
                jnp.concatenate([z[m * frame:(m + 1) * frame, :frame] for m in range(modes)], axis=1),
                jnp.concatenate([z[m * frame:(m + 1) * frame, frame:] for m in range(modes)], axis=1),
            ],
            axis=0,
        )
        y = apply_left(lf[...], z)
        power = y[:frame] * y[:frame] + y[frame:] * y[frame:]
        intensity = power[:, :frame]
        for m in range(1, modes):
            intensity = intensity + power[:, m * frame:(m + 1) * frame]
        keep = 1.0 - tgt[slot] / jnp.maximum(jnp.sqrt(intensity), 1.0)
        keep = jnp.concatenate([keep] * modes, axis=1)
        keep = jnp.concatenate([keep] * 2, axis=0)
        back = apply_left(lb[...], y * keep)
        back = jnp.concatenate(
            [
                jnp.concatenate(
                    [back[:frame, m * frame:(m + 1) * frame], back[frame:, m * frame:(m + 1) * frame]],
                    axis=1,
                )
                for m in range(modes)
            ],
            axis=0,
        )
        back = apply_right(back, rb[...])
        gr = jnp.zeros((frame, frame), jnp.float32)
        gi = jnp.zeros((frame, frame), jnp.float32)
        for m in range(modes):
            p, q = probe[m, 0], probe[m, 1]
            br = back[m * frame:(m + 1) * frame, :frame]
            bi = back[m * frame:(m + 1) * frame, frame:]
            gr = gr + (p * br + q * bi)
            gi = gi + (p * bi - q * br)
        return gr, gi

    def deposit(slot, gr, gi):
        top, lift, first, rest = place_of(slot)
        for part, g in enumerate((gr, gi)):
            wide = jnp.concatenate([g * -STEP_SIZE, jnp.zeros((SUBLANES, frame), jnp.float32)], axis=0)
            wide = pltpu.roll(wide, lift, axis=0)
            wide = jnp.concatenate([wide, jnp.zeros_like(wide)], axis=1)
            wide = pltpu.roll(wide, rest, axis=1)
            where = (part, pl.ds(top, tall), pl.ds(first, 2 * LANES))
            acc[where] = acc[where] + wide

    active = jnp.minimum(cnt[0, 0], slots)

    def pair(i, carry):
        s0 = 2 * i
        s1 = jnp.minimum(2 * i + 1, slots - 1)
        g0 = contribution(s0)
        g1 = contribution(s1)
        w = jnp.where(2 * i + 1 < active, 1.0, 0.0).astype(jnp.float32)
        deposit(s0, *g0)
        deposit(s1, g1[0] * w, g1[1] * w)
        return carry

    lax.fori_loop(0, (active + 1) // 2, pair, 0)


def frames(obj, halos, pr, pi, others, amp, pos, cnt):
    modes = lax.axis_size("mode")
    _, height, width = obj.shape
    frame = pr.shape[-1]
    slots = amp.shape[2]
    f32 = jnp.float32
    rows, cols = height + 2 * MARGIN + SUBLANES, width + 2 * LANES
    tables = [jnp.asarray(t) for t in dft_tables(frame)]
    smem = pl.BlockSpec(memory_space=pltpu.SMEM)
    anym = pl.BlockSpec(memory_space=pl.ANY)
    vmem = pl.BlockSpec(memory_space=pltpu.VMEM)
    return pl.pallas_call(
        functools.partial(frames_kernel, modes),
        out_shape=jax.ShapeDtypeStruct((2, rows, cols), f32),
        in_specs=[smem, smem] + [anym] * 8 + [vmem] * 4,
        out_specs=vmem,
        scratch_shapes=[
            pltpu.VMEM((2, rows, cols), f32),
            pltpu.VMEM((modes, 2, frame, frame), f32),
            pltpu.VMEM((slots, frame, frame), f32),
            pltpu.SemaphoreType.DMA((16,)),
            pltpu.SemaphoreType.DMA((1,)),
        ],
        name="frames",
    )(pos, cnt, obj, *halos, pr, pi, others, amp, *tables)


def fold_kernel(grad, out, got_row, got_col, got_corner, send, recv, own):
    height, width = out.shape[1], out.shape[2]
    flags = neighbour_flags()
    mine = pltpu.make_async_copy(
        grad.at[:, pl.ds(MARGIN, height), pl.ds(LANES, width)], out, own.at[0]
    )
    mine.start()
    enter(flags, [])
    parts, slots = [], []
    for a, b in DIRS:
        rs = (pl.ds(0, MARGIN), pl.ds(MARGIN, height), pl.ds(MARGIN + height, MARGIN))[a + 1]
        cs = (pl.ds(0, LANES), pl.ds(LANES, width), pl.ds(LANES + width, LANES))[b + 1]
        parts.append(grad.at[:, rs, cs])
        ia, ib = (1 - a) // 2, (1 - b) // 2
        if b == 0:
            slots.append(got_row.at[ia])
        elif a == 0:
            slots.append(got_col.at[ib])
        else:
            slots.append(got_corner.at[ia * 2 + ib])
    copies = rim_copies(parts, slots, send, recv)
    for i in range(len(DIRS)):
        @pl.when(flags[i])
        def _():
            copies[i].start()
    mine.wait()
    half = LANES - MARGIN
    for i, (a, b) in enumerate(DIRS):
        @pl.when(flags[OPP[i]])
        def _():
            copies[i].wait_recv()
            ia, ib = (1 - a) // 2, (1 - b) // 2
            r0 = (0, height - MARGIN)[ia] if a else 0
            if b == 0:
                out[:, pl.ds(r0, MARGIN), :] = out[:, pl.ds(r0, MARGIN), :] + got_row[ia]
            else:
                c0 = (0, width - LANES)[ib]
                n = MARGIN if a else height
                value = got_corner[ia * 2 + ib] if a else got_col[ib]
                out[:, pl.ds(r0, n), pl.ds(c0, LANES)] = out[:, pl.ds(r0, n), pl.ds(c0, LANES)] + value

    for i in range(len(DIRS)):
        @pl.when(flags[i])
        def _():
            copies[i].wait_send()


def fold(grad, height, width):
    f32 = jnp.float32
    sem = pltpu.SemaphoreType.DMA
    return pl.pallas_call(
        fold_kernel,
        out_shape=jax.ShapeDtypeStruct((2, height, width), f32),
        in_specs=[pl.BlockSpec(memory_space=pl.ANY)],
        out_specs=pl.BlockSpec(memory_space=pltpu.VMEM),
        scratch_shapes=[
            pltpu.VMEM((2, 2, MARGIN, width), f32),
            pltpu.VMEM((2, 2, height, LANES), f32),
            pltpu.VMEM((4, 2, MARGIN, LANES), f32),
            sem((8,)), sem((8,)), sem((1,)),
        ],
        compiler_params=pltpu.CompilerParams(collective_id=1, has_side_effects=True),
        name="fold",
    )(grad)


def per_device(object_field, probe_real, probe_imag, amplitude, positions, counts):
    *halos, others = gather(object_field, probe_real, probe_imag)
    grad = frames(object_field, halos, probe_real, probe_imag, others, amplitude, positions, counts)
    return fold(grad, object_field.shape[1], object_field.shape[2])


def solution(mesh):
    in_specs = (
        P(None, "row", "col"),
        P("mode", None, None),
        P("mode", None, None),
        P("row", "col", None, None, None),
        P("row", "col", None, None),
        P("row", "col"),
    )
    out_specs = P(None, "row", "col")
    return jax.shard_map(
        per_device, mesh=mesh, in_specs=in_specs, out_specs=out_specs, check_vma=False
    )
```

time: 186 us -> 44.1 us (0.24)
  the two profiles are of different devices: /device:TPU:1 before, /device:TPU:0 now
where the time goes in v1:
time: 44.1 us; the launch traced here: 43.4 us
  Pallas kernels  39.5 us (90%)
  local copies, waits for them, and re-layouts  3.21 us (7%)
  between operations  0.68 us (2%)
    pallas_call x1, Pallas kernels, frames(): pl.pallas_call(functools.partial(frames_kernel, modes), out_shape=jax.Sha...  17 us
    pallas_call x1, Pallas kernels, gather(): pl.pallas_call(functools.partial(gather_kernel, modes, cols), out_shape=[...  14.5 us
    pallas_call x1, Pallas kernels, fold(): pl.pallas_call(fold_kernel, out_shape=jax.ShapeDtypeStruct((2, height, wi...  7.93 us
    unnamed x2, local copies, waits for them, and re-layouts  3.21 us

profile of v1, /device:TPU:0, one launch (start us, length us, event | category | flops | bytes accessed | tf_op | source)
XLA Modules:
  0.0 43.4 jit_solution(6899203688481795449)
XLA Ops:
  0.7 1.3 %copy.11.pos = s32[1,1,8,2]{3,2,1,0:T(8,128)} copy(s32[1,1,8,2]{2,3,1,0:T(2,128)} %param.14) | data formatting | bytes 128 | tf_op args[4]
  2.0 14.5 %gather.1 = (f32[2,2,64,256]{3,2,1,0:T(8,128)}, f32[2,2,256,128]{3,2,1,0:T(8,128)}, f32[4,2,64,128]{3,2,1,0:T(8,128)}, f32[3,2,128,128]{3,2,1,0:T(8,128)}) custom-call(f32[2,256,256]{2,1,0:T(8,128)} %obj.3, f32[1,128,128]{2,1,0:T(8,128)} %pr.3, f32[1,128,128]{2,1,0:T(8,128)} %pi.3), custom_call_target="tpu_custom_call" | custom-call | tf_op jit(solution)/shard_map/gather/pallas_call | solution.py:174
  16.5 17.0 %frames.1.grad = f32[2,392,512]{2,1,0:T(8,128)} custom-call(s32[1,1,8,2]{3,2,1,0:T(8,128)} %copy.11.pos, s32[1,1]{1,0:T(1,128)S(6)} %copy.13.cnt, f32[2,256,256]{2,1,0:T(8,128)} %obj.3, f32[2,2,64,256]{3,2,1,0:T(8,128)} %get-tuple-element.9.halo_row, f32[2,2,256,128]{3,2,1,0:T(8,128)} %get-tuple-element.10.halo_col, ...), custom_call_target="tpu_custom_call" | custom-call | tf_op jit(solution)/shard_map/frames/pallas_call | solution.py:379
  33.6 7.9 %fold.1 = f32[2,256,256]{2,1,0:T(8,128)} custom-call(f32[2,392,512]{2,1,0:T(8,128)} %frames.1.grad), custom_call_target="tpu_custom_call" | custom-call | tf_op jit(solution)/shard_map/fold/pallas_call | solution.py:445
  41.5 1.9 %copy.14 = f32[2,256,256]{2,1,0:T(8,128)} copy(f32[2,256,256]{2,1,0:T(8,128)} %fold.1) | data formatting | bytes 1048576

commit v2 on v0

v2 whole, which is shorter than its diff:
```python
import functools

import jax
import jax.numpy as jnp
import numpy as np
from jax import lax
from jax.experimental import pallas as pl
from jax.experimental.pallas import tpu as pltpu
from jax.sharding import PartitionSpec as P

MARGIN = 64
LANES = 128
SUBLANES = 8
STEP_SIZE = 0.25
MESH_ID = pl.DeviceIdType.MESH

DIRS = ((-1, 0), (1, 0), (0, -1), (0, 1), (-1, -1), (-1, 1), (1, -1), (1, 1))
OPP = tuple(DIRS.index((-a, -b)) for a, b in DIRS)


def dft_tables(length):
    k = np.arange(length)
    angle = 2.0 * np.pi * (np.outer(k, k) % length) / length
    c = np.cos(angle) / np.sqrt(length)
    s = np.sin(angle) / np.sqrt(length)
    plus = np.block([[c, s], [-s, c]])
    minus = np.block([[c, -s], [s, c]])

    def split(t):
        hi = t.astype(jnp.bfloat16)
        lo = (t - hi.astype(np.float64)).astype(jnp.bfloat16)
        return hi, lo

    ph, pw = split(plus)
    mh, mw = split(minus)
    right_f = np.concatenate([mh, mh, mw], axis=0)
    left_f = np.concatenate([ph, ph, pw], axis=1)
    left_b = np.concatenate([mh, mh, mw], axis=1)
    right_b = np.concatenate([ph, ph, pw], axis=0)
    return right_f, left_f, left_b, right_b


def neighbour_flags():
    row, col = lax.axis_index("row"), lax.axis_index("col")
    rows, cols = lax.axis_size("row"), lax.axis_size("col")
    flags = []
    for a, b in DIRS:
        r, c = row + a, col + b
        ok = jnp.logical_and(jnp.logical_and(r >= 0, r < rows), jnp.logical_and(c >= 0, c < cols))
        flags.append(ok)
    return flags


def target(step):
    return (lax.axis_index("row") + step[0], lax.axis_index("col") + step[1], lax.axis_index("mode"))


def enter(flags, others):
    barrier = pltpu.get_barrier_semaphore()
    total = jnp.int32(len(others))
    for flag, step in zip(flags, DIRS):
        total = total + flag.astype(jnp.int32)

        @pl.when(flag)
        def _():
            pl.semaphore_signal(barrier, inc=1, device_id=target(step), device_id_type=MESH_ID)

    for device in others:
        pl.semaphore_signal(barrier, inc=1, device_id=device, device_id_type=MESH_ID)
    pl.semaphore_wait(barrier, total)


def rim_copies(parts, slots, send, recv):
    return [
        pltpu.make_async_remote_copy(
            src_ref=parts[i], dst_ref=slots[i], send_sem=send.at[i], recv_sem=recv.at[i],
            device_id=target(DIRS[i]), device_id_type=MESH_ID,
        )
        for i in range(len(DIRS))
    ]


def split(x):
    hi = x.astype(jnp.bfloat16)
    lo = (x - hi.astype(jnp.float32)).astype(jnp.bfloat16)
    return hi, lo


def apply_right(x, table):
    hi, lo = split(x)
    return jnp.dot(
        jnp.concatenate([hi, lo, hi], axis=1), table, preferred_element_type=jnp.float32
    )


def apply_left(table, x):
    hi, lo = split(x)
    return jnp.dot(
        table, jnp.concatenate([hi, lo, hi], axis=0), preferred_element_type=jnp.float32
    )


def step_kernel(
    modes, cols, pos, cnt, obj, pr, pi, amp, rf_in, lf_in, lb_in, rb_in,
    out,
    win, probe, tgt, patch, spec, padded, got_row, got_strip, got_corner, rim_row, strip,
    rf, lf, lb, rb,
    send, recv, csend, crecv, psend, precv, fsend, frecv, rsend, rrecv, local,
):
    row, col, mode = lax.axis_index("row"), lax.axis_index("col"), lax.axis_index("mode")
    height, width = obj.shape[1], obj.shape[2]
    frame = pr.shape[-1]
    slots = amp.shape[2]
    tall = frame + SUBLANES
    flags = neighbour_flags()
    parity = col % 2
    paired = cols % 2 == 0
    partner = col + 1 - 2 * parity
    peers = [(row, col, (mode + k) % modes) for k in range(1, modes)]
    f32 = jnp.float32

    bands = (pl.ds(0, MARGIN), pl.ds(MARGIN, height), pl.ds(MARGIN + height, MARGIN))
    strips = (pl.ds(0, LANES), pl.ds(LANES, width), pl.ds(LANES + width, LANES))

    loads = [
        (obj, win.at[:, bands[1], strips[1]]),
        (pr.at[0], probe.at[0, 0]),
        (pi.at[0], probe.at[0, 1]),
        (amp.at[0, 0], tgt),
        (rf_in, rf), (lf_in, lf), (lb_in, lb), (rb_in, rb),
    ]
    loads = [pltpu.make_async_copy(a, b, local.at[i]) for i, (a, b) in enumerate(loads)]
    for copy in loads:
        copy.start()

    enter(flags, peers)

    def probe_copy(k, side):
        return pltpu.make_async_remote_copy(
            src_ref=(pr, pi)[side].at[0], dst_ref=probe.at[k, side], send_sem=psend.at[k - 1, side],
            recv_sem=precv.at[k - 1, side], device_id=peers[k - 1], device_id_type=MESH_ID,
        )

    def forward_copy(k, side):
        return pltpu.make_async_remote_copy(
            src_ref=probe.at[k, side], dst_ref=probe.at[k, side], send_sem=fsend.at[k - 1, side],
            recv_sem=frecv.at[k - 1, side], device_id=(row, partner, mode), device_id_type=MESH_ID,
        )

    def sided(action):
        for side in (0, 1):
            if paired:
                @pl.when(parity == side)
                def _():
                    action(side)
            else:
                action(side)

    for k in range(1, modes):
        sided(lambda side: probe_copy(k, side).start())

    def side_copy(i):
        a, b = DIRS[i]
        rs = {-1: pl.ds(0, MARGIN), 0: pl.ds(0, height), 1: pl.ds(height - MARGIN, MARGIN)}[a]
        cs = {-1: pl.ds(0, LANES), 0: pl.ds(0, width), 1: pl.ds(width - LANES, LANES)}[b]
        return pltpu.make_async_remote_copy(
            src_ref=obj.at[:, rs, cs], dst_ref=win.at[:, bands[1 - a], strips[1 - b]],
            send_sem=send.at[i], recv_sem=recv.at[i], device_id=target(DIRS[i]), device_id_type=MESH_ID,
        )

    def corner_copy(i, up):
        b = DIRS[i][1]
        cs = {-1: pl.ds(LANES, LANES), 1: pl.ds(width, LANES)}[b]
        rs = bands[up + 1]
        j = (i - 2) * 2 + (up + 1) // 2
        return pltpu.make_async_remote_copy(
            src_ref=win.at[:, rs, cs], dst_ref=win.at[:, rs, strips[1 - b]],
            send_sem=csend.at[j], recv_sem=crecv.at[j], device_id=target(DIRS[i]), device_id_type=MESH_ID,
        )

    for i in range(4):
        @pl.when(flags[i])
        def _():
            side_copy(i).start()

    for i, (a, b) in enumerate(DIRS):
        @pl.when(jnp.logical_not(flags[i]))
        def _():
            place = win.at[:, bands[a + 1], strips[b + 1]]
            place[...] = jnp.zeros(place.shape, f32)

    win[:, pl.ds(2 * MARGIN + height, SUBLANES), :] = jnp.zeros((2, SUBLANES, width + 2 * LANES), f32)

    def clear(s, carry):
        padded[s] = jnp.zeros(padded.shape[1:], f32)
        return carry

    lax.fori_loop(0, slots, clear, 0)

    for copy in loads:
        copy.wait()

    for i in (0, 1):
        up = DIRS[OPP[i]][0]

        @pl.when(flags[OPP[i]])
        def _():
            side_copy(i).wait_recv()

        for j in (2, 3):
            @pl.when(jnp.logical_and(flags[OPP[i]], flags[j]))
            def _():
                corner_copy(j, up).start()

    if paired:
        for k in range(1, modes):
            def relay(side):
                probe_copy(k, side).wait_recv()
                forward_copy(k, side).start()

            sided(relay)

    for i in (2, 3):
        @pl.when(flags[OPP[i]])
        def _():
            side_copy(i).wait_recv()

        for up, r in ((-1, 0), (1, 1)):
            @pl.when(jnp.logical_and(flags[OPP[i]], flags[r]))
            def _():
                corner_copy(i, up).wait_recv()

    def place_of(slot):
        a = pos[0, 0, 0, slot]
        b = pos[0, 0, 1, slot] + (LANES - MARGIN)
        q = lax.div(b, LANES)
        top = lax.div(a, SUBLANES)
        return top, a - top * SUBLANES, q, b - q * LANES

    def cut(slot, carry):
        top, lift, q, rest = place_of(slot)
        shift = (2 * LANES - rest) % (2 * LANES)
        for part in range(2):
            wide = win[part, pl.ds(top * SUBLANES, tall), pl.ds(q * LANES, 2 * LANES)]
            wide = pltpu.roll(wide, shift, axis=1)[:, :frame]
            patch[slot, part] = pltpu.roll(wide, (tall - lift) % tall, axis=0)[:frame]
        return carry

    lax.fori_loop(0, slots, cut, 0)

    group = min(slots, 4)

    def forward(k):
        def some(g, carry):
            p, q = probe[k, 0], probe[k, 1]
            waves = []
            for j in range(group):
                re, im = patch[g * group + j, 0], patch[g * group + j, 1]
                waves.append(jnp.concatenate([p * re - q * im, p * im + q * re], axis=1))
            z = apply_right(jnp.concatenate(waves, axis=0), rf[...])
            z = jnp.concatenate(
                [
                    jnp.concatenate([z[j * frame:(j + 1) * frame, :frame] for j in range(group)], axis=1),
                    jnp.concatenate([z[j * frame:(j + 1) * frame, frame:] for j in range(group)], axis=1),
                ],
                axis=0,
            )
            y = apply_left(lf[...], z)
            for j in range(group):
                spec[k, g * group + j] = y[:, j * frame:(j + 1) * frame]
            return carry

        lax.fori_loop(0, slots // group, some, 0)

    for k in range(modes):
        if k:
            if paired:
                sided(lambda side: forward_copy(k, 1 - side).wait_recv())
            else:
                sided(lambda side: probe_copy(k, side).wait_recv())
        forward(k)

    def contribution(slot):
        y = jnp.concatenate([spec[m, slot] for m in range(modes)], axis=1)
        power = y[:frame] * y[:frame] + y[frame:] * y[frame:]
        intensity = power[:, :frame]
        for m in range(1, modes):
            intensity = intensity + power[:, m * frame:(m + 1) * frame]
        keep = 1.0 - tgt[slot] / jnp.maximum(jnp.sqrt(intensity), 1.0)
        keep = jnp.concatenate([keep] * modes, axis=1)
        keep = jnp.concatenate([keep] * 2, axis=0)
        back = apply_left(lb[...], y * keep)
        back = jnp.concatenate(
            [
                jnp.concatenate(
                    [back[:frame, m * frame:(m + 1) * frame], back[frame:, m * frame:(m + 1) * frame]],
                    axis=1,
                )
                for m in range(modes)
            ],
            axis=0,
        )
        back = apply_right(back, rb[...])
        gr = jnp.zeros((frame, frame), f32)
        gi = jnp.zeros((frame, frame), f32)
        for m in range(modes):
            p, q = probe[m, 0], probe[m, 1]
            br = back[m * frame:(m + 1) * frame, :frame]
            bi = back[m * frame:(m + 1) * frame, frame:]
            gr = gr + (p * br + q * bi)
            gi = gi + (p * bi - q * br)
        return gr, gi

    def keep_padded(slot, gr, gi):
        _, lift, _, rest = place_of(slot)
        weight = jnp.where(slot < cnt[0, 0], -STEP_SIZE, 0.0).astype(f32)
        for part, g in enumerate((gr, gi)):
            wide = jnp.concatenate([g * weight, jnp.zeros((SUBLANES, frame), f32)], axis=0)
            wide = pltpu.roll(wide, lift, axis=0)
            wide = jnp.concatenate([wide, jnp.zeros_like(wide)], axis=1)
            padded[slot, part, pl.ds(tall, tall), pl.ds(LANES, 2 * LANES)] = pltpu.roll(wide, rest, axis=1)

    def pair(i, carry):
        g0 = contribution(2 * i)
        g1 = contribution(2 * i + 1)
        keep_padded(2 * i, *g0)
        keep_padded(2 * i + 1, *g1)
        return carry

    lax.fori_loop(0, slots // 2, pair, 0)

    for j in (2, 3):
        for up, r in ((-1, 0), (1, 1)):
            @pl.when(jnp.logical_and(flags[r], flags[j]))
            def _():
                corner_copy(j, up).wait_send()

    places = [place_of(s) for s in range(slots)]

    def block_sum(part, j, t, total):
        for s in range(slots):
            top, _, q, _ = places[s]
            start = jnp.clip(tall // SUBLANES + j * (frame // SUBLANES) - top, 0, 2 * tall // SUBLANES) * SUBLANES
            lane = jnp.clip(t - q + 1, 0, 3) * LANES
            piece = padded[
                s, part, pl.ds(start, frame),
                pl.ds(lane, LANES),
            ]
            total = piece if total is None else total + piece
        return total

    n_lane = width // LANES + 2

    def rows_of(j, carry):
        r = pl.multiple_of(j * frame, frame)
        for part in range(2):
            for t in range(n_lane):
                where = (part, pl.ds(r, frame), pl.ds(t * LANES, LANES))
                edge = t in (0, n_lane - 1)
                win[where] = block_sum(part, j, t, None if edge else jnp.where(inner(j), win[where], 0.0))
        return carry

    lane_id = lax.broadcasted_iota(jnp.int32, (frame, LANES), 1)
    row_id = lax.broadcasted_iota(jnp.int32, (frame, LANES), 0)

    def inner(j):
        r = row_id + j * frame
        return jnp.logical_and(r >= MARGIN, r < MARGIN + height)

    lax.fori_loop(0, (height + 2 * MARGIN) // frame, rows_of, 0)

    for i in range(2):
        rim_row[i] = win[:, bands[2 * i], strips[1]]
    low = lax.broadcasted_iota(jnp.int32, (height + 2 * MARGIN, LANES), 1) < MARGIN
    every = pl.ds(0, height + 2 * MARGIN)
    re, im = win[0, every, strips[0]], win[1, every, strips[0]]
    strip[0] = jnp.where(low, pltpu.roll(re, MARGIN, axis=1), im)
    re, im = win[0, every, strips[2]], win[1, every, strips[2]]
    strip[1] = jnp.where(low, re, pltpu.roll(im, MARGIN, axis=1))

    parts, places_to = [], []
    for a, b in DIRS:
        if b == 0:
            parts.append(rim_row.at[(a + 1) // 2])
            places_to.append(got_row.at[(a + 1) // 2])
        elif a == 0:
            parts.append(strip.at[(b + 1) // 2, bands[1]])
            places_to.append(got_strip.at[(b + 1) // 2])
        else:
            parts.append(strip.at[(b + 1) // 2, bands[a + 1]])
            places_to.append(got_corner.at[(a + 1) + (b + 1) // 2])
    rims = rim_copies(parts, places_to, rsend, rrecv)
    for i in range(len(DIRS)):
        @pl.when(flags[i])
        def _():
            rims[i].start()

    out[...] = win[:, bands[1], strips[1]]

    def add_packed(value, b, r0, n):
        turned = pltpu.roll(value, MARGIN, axis=1)
        first = lax.broadcasted_iota(jnp.int32, (n, LANES), 1) < MARGIN
        if b < 0:
            c0, re, im, here = width - LANES, turned, value, jnp.logical_not(first)
        else:
            c0, re, im, here = 0, value, turned, first
        for part, v in enumerate((re, im)):
            where = (part, pl.ds(r0, n), pl.ds(c0, LANES))
            out[where] = out[where] + jnp.where(here, v, 0.0)

    for i, (a, b) in enumerate(DIRS):
        @pl.when(flags[OPP[i]])
        def _():
            rims[i].wait_recv()
            r0 = {-1: height - MARGIN, 0: 0, 1: 0}[a]
            if b == 0:
                where = (pl.ds(0, 2), pl.ds(r0, MARGIN), pl.ds(0, width))
                out[where] = out[where] + got_row[(a + 1) // 2]
            elif a == 0:
                add_packed(got_strip[(b + 1) // 2], b, 0, height)
            else:
                add_packed(got_corner[(a + 1) + (b + 1) // 2], b, r0, MARGIN)

    for k in range(1, modes):
        def sent(side):
            probe_copy(k, side).wait_send()
            if paired:
                forward_copy(k, side).wait_send()

        sided(sent)
    for i in range(4):
        @pl.when(flags[i])
        def _():
            side_copy(i).wait_send()
    for i in range(len(DIRS)):
        @pl.when(flags[i])
        def _():
            rims[i].wait_send()


def per_device(object_field, probe_real, probe_imag, amplitude, positions, counts):
    modes, cols = lax.axis_size("mode"), lax.axis_size("col")
    _, height, width = object_field.shape
    frame = probe_real.shape[-1]
    slots = amplitude.shape[2]
    f32 = jnp.float32
    tall = frame + SUBLANES
    tables = [jnp.asarray(t) for t in dft_tables(frame)]
    smem = pl.BlockSpec(memory_space=pltpu.SMEM)
    anym = pl.BlockSpec(memory_space=pl.ANY)
    sem = pltpu.SemaphoreType.DMA
    vmem = pltpu.VMEM
    return pl.pallas_call(
        functools.partial(step_kernel, modes, cols),
        out_shape=jax.ShapeDtypeStruct((2, height, width), f32),
        in_specs=[smem, smem] + [anym] * 8,
        out_specs=pl.BlockSpec(memory_space=vmem),
        scratch_shapes=[
            vmem((2, height + 2 * MARGIN + SUBLANES, width + 2 * LANES), f32),
            vmem((modes, 2, frame, frame), f32),
            vmem((slots, frame, frame), f32),
            vmem((slots, 2, frame, frame), f32),
            vmem((modes, slots, 2 * frame, frame), f32),
            vmem((slots, 2, 2 * tall + frame, 4 * LANES), f32),
            vmem((2, 2, MARGIN, width), f32),
            vmem((2, height, LANES), f32),
            vmem((4, MARGIN, LANES), f32),
            vmem((2, 2, MARGIN, width), f32),
            vmem((2, height + 2 * MARGIN, LANES), f32),
            *[vmem(t.shape, t.dtype) for t in tables],
            sem((4,)), sem((4,)),
            sem((4,)), sem((4,)),
            sem((modes - 1, 2)), sem((modes - 1, 2)),
            sem((modes - 1, 2)), sem((modes - 1, 2)),
            sem((8,)), sem((8,)),
            sem((8,)),
        ],
        compiler_params=pltpu.CompilerParams(collective_id=0, has_side_effects=True),
        name="gradient_step",
    )(jnp.swapaxes(positions, 2, 3), counts, object_field, probe_real, probe_imag, amplitude, *tables)


def solution(mesh):
    in_specs = (
        P(None, "row", "col"),
        P("mode", None, None),
        P("mode", None, None),
        P("row", "col", None, None, None),
        P("row", "col", None, None),
        P("row", "col"),
    )
    out_specs = P(None, "row", "col")
    return jax.shard_map(
        per_device, mesh=mesh, in_specs=in_specs, out_specs=out_specs, check_vma=False
    )
```

time: 186 us -> 41.2 us (0.22)
  the two profiles are of different devices: /device:TPU:1 before, /device:TPU:0 now
where the time goes in v2:
time: 41.2 us; the launch traced here: 41 us
  Pallas kernels  38.5 us (93%)
  local copies, waits for them, and re-layouts  1.87 us (5%)
  between operations  0.66 us (2%)
    pallas_call x1, Pallas kernels, per_device(): pl.pallas_call(functools.partial(step_kernel, modes, cols), out_shape=jax...  38.5 us
    unnamed x1, local copies, waits for them, and re-layouts  1.87 us

profile of v2, /device:TPU:0, one launch (start us, length us, event | category | flops | bytes accessed | tf_op | source)
XLA Modules:
  0.0 41.0 jit_solution(9251482453234364878)
XLA Ops:
  0.7 38.5 %gradient_step.1 = f32[2,256,256]{2,1,0:T(8,128)} custom-call(s32[1,1,2,8]{3,2,1,0:T(2,128)} %bitcast.1, s32[1,1]{1,0:T(1,128)S(6)} %copy.12.cnt, f32[2,256,256]{2,1,0:T(8,128)} %obj.1, f32[1,128,128]{2,1,0:T(8,128)} %pr.1, f32[1,128,128]{2,1,0:T(8,128)} %pi.1, f32[1,1,8,128,128]{4,3,2,1,0:T(8,128)} %amp.1, bf16[768,256]{1,0:T(8,128)(2,1)} %constant.8.clone.rf_in, ...), custom_call_target="tpu_custom_call" | custom-call | tf_op jit(solution)/shard_map/gradient_step/pallas_call | solution.py:453
  39.1 1.9 %copy.13 = f32[2,256,256]{2,1,0:T(8,128)} copy(f32[2,256,256]{2,1,0:T(8,128)} %gradient_step.1) | data formatting | bytes 1048576

commit v3 on v2

--- a/solution.py
+++ b/solution.py
@@ -251,13 +251,15 @@
     group = min(slots, 4)
 
     def forward(k):
-        def some(g, carry):
-            p, q = probe[k, 0], probe[k, 1]
+        p, q = probe[k, 0], probe[k, 1]
+        groups = []
+        for g in range(0, slots, group):
             waves = []
-            for j in range(group):
-                re, im = patch[g * group + j, 0], patch[g * group + j, 1]
+            for j in range(g, g + group):
+                re, im = patch[j, 0], patch[j, 1]
                 waves.append(jnp.concatenate([p * re - q * im, p * im + q * re], axis=1))
-            z = apply_right(jnp.concatenate(waves, axis=0), rf[...])
+            groups.append(apply_right(jnp.concatenate(waves, axis=0), rf[...]))
+        for g, z in zip(range(0, slots, group), groups):
             z = jnp.concatenate(
                 [
                     jnp.concatenate([z[j * frame:(j + 1) * frame, :frame] for j in range(group)], axis=1),
@@ -267,10 +269,7 @@
             )
             y = apply_left(lf[...], z)
             for j in range(group):
-                spec[k, g * group + j] = y[:, j * frame:(j + 1) * frame]
-            return carry
-
-        lax.fori_loop(0, slots // group, some, 0)
+                spec[k, g + j] = y[:, j * frame:(j + 1) * frame]
 
     for k in range(modes):
         if k:

time: 41.2 us -> 37.5 us (0.910)
  Pallas kernels: 38.5 us -> 34.8 us
    pallas_call x1, Pallas kernels: 38.5 us -> 34.8 us  [per_device(): pl.pallas_call(functools.partial(step_kernel, modes, cols), out_shape=jax...]
where the time goes in v3:
time: 37.5 us; the launch traced here: 37.4 us
  Pallas kernels  34.8 us (93%)
  local copies, waits for them, and re-layouts  1.87 us (5%)
  between operations  0.66 us (2%)
    pallas_call x1, Pallas kernels, per_device(): pl.pallas_call(functools.partial(step_kernel, modes, cols), out_shape=jax...  34.8 us
    unnamed x1, local copies, waits for them, and re-layouts  1.87 us

profile of v3, /device:TPU:0, one launch (start us, length us, event | category | flops | bytes accessed | tf_op | source)
XLA Modules:
  0.0 37.4 jit_solution(13558071104841921355)
XLA Ops:
  0.7 34.8 %gradient_step.1 = f32[2,256,256]{2,1,0:T(8,128)} custom-call(s32[1,1,2,8]{3,2,1,0:T(2,128)} %bitcast.1, s32[1,1]{1,0:T(1,128)S(6)} %copy.12.cnt, f32[2,256,256]{2,1,0:T(8,128)} %obj.1, f32[1,128,128]{2,1,0:T(8,128)} %pr.1, f32[1,128,128]{2,1,0:T(8,128)} %pi.1, f32[1,1,8,128,128]{4,3,2,1,0:T(8,128)} %amp.1, bf16[768,256]{1,0:T(8,128)(2,1)} %constant.8.clone.rf_in, ...), custom_call_target="tpu_custom_call" | custom-call | tf_op jit(solution)/shard_map/gradient_step/pallas_call | solution.py:452
  35.5 1.9 %copy.13 = f32[2,256,256]{2,1,0:T(8,128)} copy(f32[2,256,256]{2,1,0:T(8,128)} %gradient_step.1) | data formatting | bytes 1048576

commit v4 on v3

--- a/solution.py
+++ b/solution.py
@@ -319,14 +319,13 @@
             wide = jnp.concatenate([wide, jnp.zeros_like(wide)], axis=1)
             padded[slot, part, pl.ds(tall, tall), pl.ds(LANES, 2 * LANES)] = pltpu.roll(wide, rest, axis=1)
 
-    def pair(i, carry):
-        g0 = contribution(2 * i)
-        g1 = contribution(2 * i + 1)
-        keep_padded(2 * i, *g0)
-        keep_padded(2 * i + 1, *g1)
+    def some(i, carry):
+        found = [contribution(group * i + j) for j in range(group)]
+        for j, g in enumerate(found):
+            keep_padded(group * i + j, *g)
         return carry
 
-    lax.fori_loop(0, slots // 2, pair, 0)
+    lax.fori_loop(0, slots // group, some, 0)
 
     for j in (2, 3):
         for up, r in ((-1, 0), (1, 1)):

time: 37.5 us -> 35.9 us (0.957)
  Pallas kernels: 34.8 us -> 33.2 us
    pallas_call x1, Pallas kernels: 34.8 us -> 33.2 us  [per_device(): pl.pallas_call(functools.partial(step_kernel, modes, cols), out_shape=jax...]
where the time goes in v4:
time: 35.9 us; the launch traced here: 35.7 us
  Pallas kernels  33.2 us (92%)
  local copies, waits for them, and re-layouts  1.87 us (5%)
  between operations  0.66 us (2%)
    pallas_call x1, Pallas kernels, per_device(): pl.pallas_call(functools.partial(step_kernel, modes, cols), out_shape=jax...  33.2 us
    unnamed x1, local copies, waits for them, and re-layouts  1.87 us

profile of v4, /device:TPU:0, one launch (start us, length us, event | category | flops | bytes accessed | tf_op | source)
XLA Modules:
  0.0 35.7 jit_solution(8146154080649832995)
XLA Ops:
  0.7 33.2 %gradient_step.1 = f32[2,256,256]{2,1,0:T(8,128)} custom-call(s32[1,1,2,8]{3,2,1,0:T(2,128)} %bitcast.1, s32[1,1]{1,0:T(1,128)S(6)} %copy.12.cnt, f32[2,256,256]{2,1,0:T(8,128)} %obj.1, f32[1,128,128]{2,1,0:T(8,128)} %pr.1, f32[1,128,128]{2,1,0:T(8,128)} %pi.1, f32[1,1,8,128,128]{4,3,2,1,0:T(8,128)} %amp.1, bf16[768,256]{1,0:T(8,128)(2,1)} %constant.8.clone.rf_in, ...), custom_call_target="tpu_custom_call" | custom-call | tf_op jit(solution)/shard_map/gradient_step/pallas_call | solution.py:451
  33.9 1.9 %copy.13 = f32[2,256,256]{2,1,0:T(8,128)} copy(f32[2,256,256]{2,1,0:T(8,128)} %gradient_step.1) | data formatting | bytes 1048576
